TPU v7x, 256 devices: a whole 4x4x8 slice. The times are simulated.
256 devices in a mesh: req: 64 (over z, y, core), tp: 4 (over x).
Axes of the slice: x: 4, y: 4, z: 8, core: 2. Of those that a mesh axis runs over, the one named last changes fastest.
Arguments:
- drafts: bfloat16 [128, 64, 1536], P('req'), may hold values from -27 to 27, as said below
- gain_attn: float32 [1536], replicated, may hold values from 0.1 to 1.9
- w_query: bfloat16 [1536, 1536], P(None, 'tp'), may hold values from -0.15625 to 0.15625
- key_value_weight: bfloat16 [1536, 512], replicated, may hold values from -0.15625 to 0.15625
- w_output: bfloat16 [1536, 1536], P('tp'), may hold values from -0.5 to 0.5
- cache: bfloat16 [128, 2, 2, 3072, 128], P('req'), may hold values from -130 to 130, as said below
- lengths: int32 [128], P('req'), may hold values from 1 to 3072, 131072 in all
- tree_mask: int32 [128, 64, 64], P('req'), may hold values from 0 to 1, as said below
- depths: int32 [128, 64], P('req'), may hold values from 0 to 63, as said below
- gain_moe: float32 [1536], replicated, may hold values from 0.1 to 1.9
- w_router: bfloat16 [1536, 32], replicated, may hold values from -0.15625 to 0.15625
- expert_ids: int32 [128, 64, 4], P('req'), may hold values from 0 to 31, all different within a row; in each aligned block of 128 rows (0 to 127, 128 to 255, ..., all dimensions but the last counted through in order) at most 32 rows name the same one
- w_in: bfloat16 [64, 1536, 2, 384], P('req'), may hold values from -0.15625 to 0.15625
- w_out: bfloat16 [64, 384, 1536], P('req'), may hold values from -0.21875 to 0.21875
- slots: int32 [128, 64], P('req'), may hold values from -1 to 15, as said below
- order: int32 [128], P('req'), may hold values from 0 to 127, each once
Outputs:
- tree_out: bfloat16 [128, 64, 1536], P('req', None, 'tp')
- accepted: bfloat16 [128, 16, 1536], P('req', None, 'tp')
Inputs may be any that keep to these rules, and one draw needn't show every extreme that they name: `drafts`: values lie within this range. `cache`: values lie within this range. `tree_mask`: each request's tokens form a tree rooted at token 0, the parent of token t being one of tokens t - 4 to t - 1; entry [s, i, j] is 1 exactly when j is i or an ancestor of i. `depths`: depth of each token in its tree, agreeing with tree_mask; the root has depth 0. In every draw some request's tree is a single chain. In each request the tokens on the path from the root to one token of depth d carry slots 0 to d (their depths), with d + 1 <= 16; all other tokens carry -1. In every draw some request fills all 16 slots. `expert_ids`: each token names 4 different experts; among the tokens of one device no expert is named by more than 32 tokens. `order`: each request is served in exactly one serving slot.
All inputs are finite; a program needn't handle non-finite values. No bound on the sum of `lengths` on one device may be relied on, other than what follows from the above.
Results may differ from a plain program's by a relative error of at most 0.011.
Values may be sent and summed in bfloat16 or wider, within the bound.
A program may use at most 64 MiB of HBM per device.

v0:
```python
import jax
import jax.numpy as jnp
from jax import lax
from jax.sharding import PartitionSpec as P

KEEP = 16
CAP = 32


EPSILON = 1e-06
THETA = 1000000.0


def rms_norm(values, gain_vec):
    return (
        values * lax.rsqrt(jnp.mean(values * values, axis=-1, keepdims=True) + EPSILON) * gain_vec
    )


def rotary(values, positions):
    half_dim = values.shape[-1] // 2
    freqs = jnp.exp(-jnp.log(THETA) * jnp.arange(half_dim, dtype=jnp.float32) / half_dim)
    angles = positions.astype(jnp.float32)[..., None] * freqs
    cosine = jnp.cos(angles)
    sine = jnp.sin(angles)
    first = values[..., :half_dim]
    second = values[..., half_dim:]
    return jnp.concatenate(
        [first * cosine - second * sine, second * cosine + first * sine], axis=-1
    )


def inner_rows(left, right):
    return lax.dot_general(
        left, right, (((1,), (1,)), ((), ())), preferred_element_type=jnp.float32
    )


def cache_block(cache, request, which, kv_head, offset, block_len):
    head_dim = cache.shape[-1]
    found = lax.dynamic_slice(
        cache, (request, which, kv_head, offset, 0), (1, 1, 1, block_len, head_dim)
    )
    return found.reshape(block_len, head_dim)


def block_scores(cache, queries, request, kv_head, offset, block_len, limit, scale):
    keys_blk = cache_block(cache, request, 0, kv_head, offset, block_len)
    scores = inner_rows(queries, keys_blk) * scale
    inside = offset + jnp.arange(block_len) < limit
    return jnp.where(inside[None, :], scores, -jnp.inf)


def attend_request(cache, queries, key_tree, val_tree, allowed, limit, request, kv_head, scale):
    block_len = min(512, cache.shape[3])
    tree_scores = jnp.where(allowed, inner_rows(queries, key_tree) * scale, -jnp.inf)
    count_blocks = (limit + block_len - 1) // block_len

    def max_step(blk_index, running):
        scores = block_scores(
            cache, queries, request, kv_head, blk_index * block_len, block_len, limit, scale
        )
        return jnp.maximum(running, jnp.max(scores, axis=1))

    peak = lax.fori_loop(0, count_blocks, max_step, jnp.max(tree_scores, axis=1))
    tree_weights = jnp.exp(tree_scores - peak[:, None])
    start_carry = (
        jnp.sum(tree_weights, axis=1),
        jnp.dot(tree_weights.astype(jnp.bfloat16), val_tree, preferred_element_type=jnp.float32),
    )

    def sum_step(blk_index, carry):
        weight_sum, accum = carry
        offset = blk_index * block_len
        scores = block_scores(cache, queries, request, kv_head, offset, block_len, limit, scale)
        weights = jnp.exp(scores - peak[:, None])
        vals_blk = cache_block(cache, request, 1, kv_head, offset, block_len)
        return (
            weight_sum + jnp.sum(weights, axis=1),
            accum
            + jnp.dot(weights.astype(jnp.bfloat16), vals_blk, preferred_element_type=jnp.float32),
        )

    weight_sum, accum = lax.fori_loop(0, count_blocks, sum_step, start_carry)
    return (accum / weight_sum[:, None]).astype(jnp.bfloat16)


def on_device(
    drafts,
    gain_attn,
    w_query,
    key_value_weight,
    w_output,
    cache,
    lengths,
    tree_mask,
    depths,
    gain_moe,
    w_router,
    expert_ids,
    w_in,
    w_out,
    slots,
    order,
):
    req_dev, draft_tree, width = drafts.shape
    head_dim = cache.shape[-1]
    kv_heads = cache.shape[2]
    local_heads = w_query.shape[1] // head_dim
    tp_count = lax.axis_size("tp")
    req_count = lax.axis_size("req")
    tp_rank = lax.axis_index("tp")
    head_group = local_heads * tp_count // kv_heads
    kv_head = tp_rank * local_heads // head_group
    scale = head_dim ** (-0.5)
    tokens = req_dev * draft_tree
    inputs = drafts.astype(jnp.float32).reshape(tokens, width)
    normalized_input = rms_norm(inputs, gain_attn).astype(jnp.bfloat16)
    positions = lengths[:, None] + depths
    query_rot = jnp.dot(normalized_input, w_query, preferred_element_type=jnp.float32).reshape(
        req_dev, draft_tree, local_heads, head_dim
    )
    query_rot = rotary(query_rot, positions[:, :, None]).astype(jnp.bfloat16)
    key_value = jnp.dot(
        normalized_input, key_value_weight, preferred_element_type=jnp.float32
    ).reshape(req_dev, draft_tree, 2, kv_heads, head_dim)
    keyval_own = lax.dynamic_index_in_dim(key_value, kv_head, 3, keepdims=False)
    key_new = rotary(keyval_own[:, :, 0], positions).astype(jnp.bfloat16)
    val_new = keyval_own[:, :, 1].astype(jnp.bfloat16)
    head_rows = []
    for request in range(req_dev):
        queries = query_rot[request].transpose(1, 0, 2).reshape(local_heads * draft_tree, head_dim)
        allowed = jnp.tile(tree_mask[request] > 0, (local_heads, 1))
        mixed = attend_request(
            cache,
            queries,
            key_new[request],
            val_new[request],
            allowed,
            lengths[request],
            request,
            kv_head,
            scale,
        )
        head_rows.append(
            mixed.reshape(local_heads, draft_tree, head_dim)
            .transpose(1, 0, 2)
            .reshape(draft_tree, local_heads * head_dim)
        )
    heads = jnp.concatenate(head_rows, axis=0)
    attn = lax.psum(
        jnp.dot(heads, w_output, preferred_element_type=jnp.float32).astype(jnp.bfloat16), "tp"
    ).astype(jnp.float32)
    resid = inputs + attn
    normed2 = rms_norm(resid, gain_moe).astype(jnp.bfloat16)
    experts = w_router.shape[1]
    logits = jnp.dot(normed2, w_router, preferred_element_type=jnp.float32)
    ids = expert_ids.reshape(tokens, -1)
    picks = ids[:, :, None] == jnp.arange(experts)[None, None, :]
    chosen = jax.nn.sigmoid(jnp.sum(jnp.where(picks, logits[:, None, :], 0.0), axis=-1))
    gates = (chosen / jnp.sum(chosen, axis=1, keepdims=True)).astype(jnp.bfloat16)
    counts = jnp.sum(picks.astype(jnp.int32), axis=1)
    slot_expert = jnp.cumsum(counts, axis=0) - counts
    slot_pick = jnp.sum(jnp.where(picks, slot_expert[:, None, :], 0), axis=-1)
    share = CAP // tp_count
    first_slot = tp_rank * share
    cap_index = first_slot + jnp.arange(share)
    dispatch_mat = (
        (counts.T[:, None, :] == 1) & (slot_expert.T[:, None, :] == cap_index[None, :, None])
    ).astype(jnp.bfloat16)
    sent = jnp.einsum(
        "ect,td->ecd", dispatch_mat, normed2, preferred_element_type=jnp.float32
    ).astype(jnp.bfloat16)
    pieces = w_in.shape[0]
    outgoing = jnp.repeat(sent, 2, axis=0).reshape(req_count, pieces, share, width)
    arrived = lax.all_to_all(outgoing, "req", split_axis=0, concat_axis=0, tiled=True)
    rows_in = arrived.transpose(1, 0, 2, 3).reshape(pieces, req_count * share, width)
    gate_up = jnp.einsum("prd,pdgf->prgf", rows_in, w_in, preferred_element_type=jnp.float32)
    act = (jax.nn.relu(gate_up[:, :, 0]) * gate_up[:, :, 1]).astype(jnp.bfloat16)
    produced = jnp.einsum("prf,pfd->prd", act, w_out, preferred_element_type=jnp.float32).astype(
        jnp.bfloat16
    )
    outbound = produced.reshape(pieces, req_count, share, width).transpose(1, 0, 2, 3)
    returned = lax.all_to_all(outbound, "req", split_axis=0, concat_axis=0, tiled=True)
    expert_rows = returned.reshape(experts * 2 * share, width)
    local_slot = slot_pick - first_slot
    owned = (local_slot >= 0) & (local_slot < share)
    target = jnp.where(owned, ids * share + local_slot, -1)
    combine_one = jnp.sum(
        jnp.where(
            target[:, :, None] == jnp.arange(experts * share)[None, None, :],
            gates[:, :, None],
            jnp.zeros((), jnp.bfloat16),
        ),
        axis=1,
    )
    combine = jnp.broadcast_to(
        combine_one.reshape(tokens, experts, 1, share), (tokens, experts, 2, share)
    ).reshape(tokens, experts * 2 * share)
    quarter = width // tp_count
    mixture = lax.psum_scatter(
        lax.dot_general(
            expert_rows, combine, (((0,), (1,)), ((), ())), preferred_element_type=jnp.float32
        ).astype(jnp.bfloat16),
        "tp",
        scatter_dimension=0,
        tiled=True,
    ).astype(jnp.float32)
    own_resid = lax.dynamic_slice_in_dim(resid, tp_rank * quarter, quarter, 1)
    tree_out = (own_resid + mixture.T).astype(jnp.bfloat16).reshape(req_dev, draft_tree, quarter)
    selector = (slots[:, None, :] == jnp.arange(KEEP)[None, :, None]).astype(jnp.bfloat16)
    kept_rows = jnp.einsum(
        "rkt,rtd->rkd", selector, tree_out, preferred_element_type=jnp.float32
    ).astype(jnp.bfloat16)
    destination = (order[:, None] == jnp.arange(req_count * req_dev)[None, :]).astype(jnp.bfloat16)
    posted = jnp.einsum(
        "rg,rkd->gkd", destination, kept_rows, preferred_element_type=jnp.float32
    ).astype(jnp.bfloat16)
    received = lax.all_to_all(
        posted.reshape(req_count, req_dev, KEEP, quarter),
        "req",
        split_axis=0,
        concat_axis=0,
        tiled=True,
    )
    accepted = jnp.sum(received.astype(jnp.float32), axis=0).astype(jnp.bfloat16)
    return (tree_out, accepted)


def solution(mesh):
    placed = (
        P("req", None, None),
        P(),
        P(None, "tp"),
        P(),
        P("tp", None),
        P("req", None, None, None, None),
        P("req"),
        P("req", None, None),
        P("req", None),
        P(),
        P(),
        P("req", None, None),
        P("req", None, None, None),
        P("req", None, None),
        P("req", None),
        P("req"),
    )
    return jax.shard_map(
        on_device,
        mesh=mesh,
        in_specs=placed,
        out_specs=(P("req", None, "tp"), P("req", None, "tp")),
        check_vma=False,
    )
```

profile of v0, /device:TPU:1, one launch (start us, length us, event | category | flops | bytes accessed | tf_op | source)
XLA Modules:
  0.0 325.0 jit_solution(3693844473120576054)
XLA Ops:
  7.3 1.4 fusion.101
  11.2 2.7 copy.81
  13.8 2.1 fusion.51
  16.0 2.5 copy.60
  18.5 1.8 fusion.53
  21.3 11.4 %while.52 = (s32[]{:T(128)}, f32[192]{0:T(256)S(1)}, s32[]{:T(128)}, s32[]{:T(128)}, bf16[2,2,2,3072,128]{4,3,2,1,0:T(8,128)(2,1)}, /*index=5*/s32[]{:T(128)}, b...) while((s32[]{:T(128)}, f32[192]{0:T(256)S(1)}, s32[]{:T(128)}, ...), condition=%wide.region_4.5_spmd, body=%wide.region_2.4_spmd.sunk | while | flops 25461764 | bytes 184999 | solution.py:65
  33.3 3.7 %while.54 = (s32[]{:T(128)}, f32[192]{0:T(256)S(1)}, s32[]{:T(128)}, s32[]{:T(128)}, bf16[2,2,2,3072,128]{4,3,2,1,0:T(8,128)(2,1)}, /*index=5*/s32[]{:T(128)}, b...) while((s32[]{:T(128)}, f32[192]{0:T(256)S(1)}, s32[]{:T(128)}, ...), condition=%wide.region_12.13_spmd, body=%wide.region_10.12_spmd.sunk | while | flops 25461764 | bytes 184999 | solution.py:65
  34.0 1.2 fusion.141
  37.3 18.3 %while.53 = (s32[]{:T(128)}, f32[192]{0:T(256)S(1)}, f32[192,128]{1,0:T(8,128)S(1)}, s32[]{:T(128)}, s32[]{:T(128)}, /*index=5*/bf16[2,2,2,3072,128]{4,3,2,1,0:T...) while((s32[]{:T(128)}, f32[192]{0:T(256)S(1)}, ...), condition=%wide.region_8.9_spmd, body=%wide.region_6.8_spmd.sunk | while | flops 50848772 | bytes 907195 | solution.py:84
  38.0 1.3 fusion.138
  41.0 1.3 fusion.138
  44.1 1.3 fusion.138
  47.2 1.3 fusion.138
  50.2 1.3 fusion.138
  53.3 1.3 fusion.138
  55.8 6.1 %while.55 = (s32[]{:T(128)}, f32[192]{0:T(256)S(1)}, f32[192,128]{1,0:T(8,128)S(1)}, s32[]{:T(128)}, s32[]{:T(128)}, /*index=5*/bf16[2,2,2,3072,128]{4,3,2,1,0:T...) while((s32[]{:T(128)}, f32[192]{0:T(256)S(1)}, ...), condition=%wide.region_16.17_spmd, body=%wide.region_14.16_spmd.sunk | while | flops 50848772 | bytes 907195 | solution.py:84
  56.5 1.3 fusion.145
  59.5 1.2 fusion.145
  62.1 2.4 convolution_convert_fusion.3
  66.6 62.2 %all-reduce.2.cloned.1.call-done = bf16[128,1536]{1,0:T(8,128)(2,1)} async-done(((bf16[128,1536]{1,0:T(8,128)(2,1)}), bf16[128,1536]{1,0:T(8,128)(2,1)}) %all-reduce.2.cloned.1.call-update) | async-done | bytes 393232 | tf_op jit(solution)/shard_map/psum | solution.py:151
  131.3 51.7 %all_to_all.15 = bf16[64,1,8,1536]{3,2,1,0:T(8,128)(2,1)S(1)} all-to-all(bf16[64,1,8,1536]{3,2,1,0:T(8,128)(2,1)S(1)} %bitcast.179), channel_id=1, replica_groups=mesh['req'=64,'tp'=4] {'req'}, dimensions={0} | all-to-all | bytes 3145728 | tf_op jit(solution)/shard_map/all_to_all | solution.py:176
  183.0 1.4 fusion.39
  184.4 2.1 fusion.34
  186.6 6.7 %all-to-all-start.1 = ((bf16[64,1,8,1536]{3,2,1,0:T(8,128)(2,1)}), bf16[64,1,8,1536]{3,2,1,0:T(8,128)(2,1)}, u32[]{:S(2)}, u32[]{:S(2)}) async-start(bf16[64,1,8,1536]{3,2,1,0:T(8,128)(2,1)} %fusion.34), calls=%async_computation.1 | async-start | bytes 3145728 | tf_op jit(solution)/shard_map/all_to_all | solution.py:184
  194.4 37.9 %all-to-all-done.1 = bf16[64,1,8,1536]{3,2,1,0:T(8,128)(2,1)} async-done(((bf16[64,1,8,1536]{3,2,1,0:T(8,128)(2,1)}), bf16[64,1,8,1536]{3,2,1,0:T(8,128)(2,1)}, u32[]{:S(2)}, u32[]{:S(2)}) %all-to-all-start.1) | async-done | bytes 1572896 | tf_op jit(solution)/shard_map/all_to_all | solution.py:184
  232.3 2.8 convolution_convert_fusion.2
  235.1 17.7 %reduce-scatter.4.cloned.1.call-done = bf16[384,128]{1,0:T(8,128)(2,1)} async-done(((bf16[1536,128]{1,0:T(8,128)(2,1)}), bf16[384,128]{1,0:T(8,128)(2,1)}) %reduce-scatter.4.cloned.1.call-update) | async-done | bytes 98320
  254.0 1.8 convolution_convert_fusion.4
  255.8 4.5 %reshape.282 = bf16[64,2,16,384]{3,1,0,2:T(2,128)(2,1)} reshape(bf16[128,16,384]{2,0,1:T(8,128)(2,1)} %convolution_convert_fusion.4) | data formatting | bytes 3145728 | tf_op jit(solution)/shard_map/reshape | solution.py:220
  260.3 2.5 copy.76
  262.8 52.1 %all_to_all.16 = bf16[64,2,16,384]{3,1,2,0:T(2,128)(2,1)} all-to-all(bf16[64,2,16,384]{3,1,2,0:T(2,128)(2,1)S(1)} %copy.76), channel_id=1, replica_groups=mesh['req'=64,'tp'=4] {'req'}, dimensions={0} | all-to-all | bytes 3145728 | tf_op jit(solution)/shard_map/all_to_all | solution.py:219
  314.9 2.7 reduce_sum.127
  (141 shorter events, 38.5 us)
Async XLA Ops:
  7.2 175.9 %copy-start = (bf16[1,1536,2,384]{3,2,1,0:T(2,128)(2,1)S(1)}, bf16[1,1536,2,384]{3,2,1,0:T(2,128)(2,1)}, u32[]{:S(2)}) copy-start(bf16[1,1536,2,384]{3,2,1,0:T(2,128)(2,1)} %param.36) | copy-start | bytes 7077892
  7.2 121.6 %all-reduce.2.cloned.1.call-start = ((), (), s32[]{:S(2)}) async-start(), calls=%async_computation.4 | async-start | bytes 786432 | tf_op jit(solution)/shard_map/psum | solution.py:151
  11.1 2.7 copy-start.1
  11.1 2.7 copy-start.7
  13.8 2.1 copy-start.13
  13.8 2.1 copy-start.16
  16.0 4.3 %copy-start.8 = (s32[2,64,64]{2,1,0:T(8,128)S(1)}, s32[2,64,64]{2,1,0:T(8,128)}, u32[]{:S(2)}) copy-start(s32[2,64,64]{2,1,0:T(8,128)} %param.31) | copy-start | bytes 98308
  61.9 2.6 copy-start.14
  64.6 0.6 copy-start.9
  65.4 1.3 copy-start.3
  128.8 1.2 copy-start.12
  128.8 1.2 copy-start.18
  183.0 1.4 copy-start.2
  186.6 6.9 %copy-start.4 = (s32[128,32]{1,0:T(8,128)S(1)}, s32[128,32]{1,0:T(8,128)}, u32[]{:S(2)}) copy-start(s32[128,32]{1,0:T(8,128)} %copy-done.3) | copy-start | bytes 49156
  186.6 7.0 %copy-start.10 = (s32[128,4]{0,1:T(4,128)S(1)}, s32[128,4]{0,1:T(4,128)}, u32[]{:S(2)}) copy-start(s32[128,4]{0,1:T(4,128)} %copy-done.9) | copy-start | bytes 6148
  186.6 7.1 %copy-start.6 = (bf16[1536,32]{0,1:T(8,128)(2,1)S(1)}, bf16[1536,32]{0,1:T(8,128)(2,1)}, u32[]{:S(2)}) copy-start(bf16[1536,32]{0,1:T(8,128)(2,1)} %param.34) | copy-start | bytes 294916
  186.6 7.1 %copy-start.11 = (f32[1536]{0:T(1024)S(1)}, f32[1536]{0:T(1024)}, u32[]{:S(2)}) copy-start(f32[1536]{0:T(1024)} %param.33) | copy-start | bytes 18436
  186.6 45.7 %all-to-all-start.1 = ((bf16[64,1,8,1536]{3,2,1,0:T(8,128)(2,1)}), bf16[64,1,8,1536]{3,2,1,0:T(8,128)(2,1)}, u32[]{:S(2)}, u32[]{:S(2)}) async-start(bf16[64,1,8,1536]{3,2,1,0:T(8,128)(2,1)} %fusion.34), calls=%async_computation.1 | async-start | bytes 3145728 | tf_op jit(solution)/shard_map/all_to_all | solution.py:184
  193.3 59.5 %reduce-scatter.4.cloned.1.call-start = ((), (), s32[]{:S(2)}) async-start(), calls=%async_computation.5 | async-start | bytes 491520
  232.3 21.6 %copy-start.15 = (s32[2,64]{1,0:T(2,128)S(1)}, s32[2,64]{1,0:T(2,128)}, u32[]{:S(2)}) copy-start(s32[2,64]{1,0:T(2,128)} %param.38) | copy-start | bytes 1540
  232.3 21.7 %copy-start.17 = (s32[2]{0:T(128)S(1)}, s32[2]{0:T(128)}, u32[]{:S(2)}) copy-start(s32[2]{0:T(128)} %param.39) | copy-start | bytes 28
  253.8 6.5 %copy-start.5 = (bf16[128,384]{1,0:T(8,128)(2,1)}, bf16[128,384]{1,0:T(8,128)(2,1)S(1)}, u32[]{:S(2)}) copy-start(bf16[128,384]{1,0:T(8,128)(2,1)S(1)} %fusion.58) | copy-start | bytes 294916
Sparse Core Ops, SparseCore 0:
  64.6 64.1 all-reduce.1
  235.2 17.5 reduce-scatter.3
where the time goes:
time: 329 us; the launch traced here: 325 us
  waiting for transfers between devices  118 us (36%)
  blocking collectives  104 us (32%)
  matrix products  45.4 us (14%)
  other arithmetic  18.1 us (6%)
  local copies, waits for them, and re-layouts  16.6 us (5%)
  between operations  15.8 us (5%)
  starting transfers between devices  6.94 us (2%)
    psum x1, waiting for transfers between devices, on_device(): lax.psum(jnp.dot(heads, w_output, preferred_element_type=jnp.float32).ast...  62.2 us
    all_to_all x1, blocking collectives, on_device(): lax.all_to_all(posted.reshape(req_count, req_dev, KEEP, quarter), 'req',...  52.1 us
    all_to_all x1, blocking collectives, on_device(): lax.all_to_all(outgoing, 'req', split_axis=0, concat_axis=0, tiled=True)  51.7 us
    all_to_all x1, waiting for transfers between devices, on_device(): lax.all_to_all(outbound, 'req', split_axis=0, concat_axis=0, tiled=True)  37.9 us
    dot_general x18, matrix products, inner_rows(): lax.dot_general(left, right, (((1,), (1,)), ((), ())), preferred_element_...  20.2 us
    unnamed x3, waiting for transfers between devices  17.7 us
    lt x16, other arithmetic, block_scores(): inside = offset + jnp.arange(block_len) < limit  10.1 us
    dot_general x8, matrix products, sum_step(): jnp.dot(weights.astype(jnp.bfloat16), vals_blk, preferred_element_type=jn...  8.87 us
  transfers between devices with their start and end apart: 3, of which 3 were waited for; matrix products, arithmetic and copies ran while one was open for 1% of the time, Pallas kernels for 0%

commit v1 on v0

v1 whole, which is shorter than its diff:
```python
import jax
import jax.numpy as jnp
from jax import lax
from jax.experimental import pallas as pl
from jax.experimental.pallas import tpu as pltpu
from jax.sharding import PartitionSpec as P

KEEP = 16
EPSILON = 1e-06
THETA = 1000000.0
NX = 4
NY = 4
NZ = 8
CHIPS = 32
SHARE = 8
HEAD = 128
HEADS = 3
TREE = 64
TOKENS = 128
WIDTH = 1536
QUARTER = 384
LONGEST = 3072
BLOCK = 512
HALF_FF = 384
PEERS = 38
BATCHES = ((0, 4), (1, 7), (2, 6), (3, 5))
SEND_ORDER = (1, 7, 2, 6, 3, 5, 4, 0)
F32 = jnp.float32
BF16 = jnp.bfloat16
MESH = pl.DeviceIdType.MESH


def mm(left, right):
    return jnp.dot(left, right, preferred_element_type=F32)


def mm_nt(left, right):
    return lax.dot_general(left, right, (((1,), (1,)), ((), ())), preferred_element_type=F32)


def mm_tn(left, right):
    return lax.dot_general(left, right, (((0,), (0,)), ((), ())), preferred_element_type=F32)


def iota(shape, dim):
    return lax.broadcasted_iota(jnp.int32, shape, dim)


def to_rows(blocks):
    shape = blocks.shape
    rows = 1
    for size in shape[:-1]:
        rows *= size
    return blocks.astype(F32).reshape(rows, shape[-1]).astype(BF16)


def wait_for(ref, sem):
    pltpu.make_async_copy(ref, ref, sem).wait()


def layer(
    drafts_h,
    gain_attn_h,
    w_query_h,
    kv_weight_h,
    w_output_h,
    cache_h,
    lengths_s,
    tree_mask_h,
    depths_h,
    gain_moe_h,
    w_router_h,
    ids_h,
    w_in_h,
    w_out_h,
    slots_h,
    order_s,
    tree_out_ref,
    accepted_ref,
    drafts,
    gain_attn,
    w_qkv,
    w_output,
    kbuf,
    vbuf,
    tree_mask,
    depths,
    gain_moe,
    w_router,
    ids,
    w_in_raw,
    w_in,
    w_out,
    slots,
    load_sem,
    rs_send,
    rs_recv,
    rs_ssem,
    rs_rsem,
    ag_all,
    ag_ssem,
    ag_rsem,
    dmat,
    comb,
    normed2,
    send_buf,
    rows,
    own_part,
    sib_send,
    sib_recv,
    ret_send,
    ret,
    disp_ssem,
    disp_rsem,
    relay_ssem,
    relay_rsem,
    sib_ssem,
    sib_rsem,
    ret_ssem,
    ret_rsem,
    mix_send,
    mix_recv,
    mix_ssem,
    mix_rsem,
    ord_all,
    ord_ssem,
    ord_rsem,
    z_all,
    z_ssem,
    z_rsem,
    yc_send,
    yc_recv,
    yc_ssem,
    yc_rsem,
):
    x = lax.axis_index("tp")
    req = lax.axis_index("req")
    core = req % 2
    chip = req // 2
    y = chip % NY
    z = chip // NY
    kv_head = x // 2
    other = 1 - core

    def place(zz, yy, cc):
        return ((zz * NY + yy) * 2 + cc, x)

    barrier = pltpu.get_barrier_semaphore()

    def greet(device):
        pl.semaphore_signal(barrier, inc=1, device_id=device, device_id_type=MESH)

    for dx in range(1, NX):
        greet((req, (x + dx) % NX))
    for dz in range(NZ):
        for dy in range(NY):
            if dz or dy:
                greet(place((z + dz) % NZ, (y + dy) % NY, core))
    for dy in range(NY):
        greet(place(z, (y + dy) % NY, other))

    loads = []

    def load(source, target):
        copy = pltpu.make_async_copy(source, target, load_sem.at[len(loads)])
        copy.start()
        loads.append(copy)
        return copy

    l_drafts = load(drafts_h, drafts)
    l_gain = load(gain_attn_h, gain_attn)
    l_depths = load(depths_h, depths)
    l_wq = load(w_query_h, w_qkv.at[:, pl.ds(0, QUARTER)])
    l_wk = load(
        kv_weight_h.at[:, pl.ds(pl.multiple_of(kv_head * HEAD, HEAD), HEAD)],
        w_qkv.at[:, pl.ds(QUARTER, HEAD)],
    )
    l_wv = load(
        kv_weight_h.at[:, pl.ds(pl.multiple_of(256 + kv_head * HEAD, HEAD), HEAD)],
        w_qkv.at[:, pl.ds(QUARTER + HEAD, HEAD)],
    )
    l_mask = load(tree_mask_h, tree_mask)
    l_cache = []
    for request in range(2):
        l_cache.append(load(cache_h.at[request, 0, kv_head], kbuf.at[request]))
        l_cache.append(load(cache_h.at[request, 1, kv_head], vbuf.at[request]))
    l_wo = load(w_output_h, w_output)
    l_ids = load(ids_h, ids)
    l_win = load(w_in_h, w_in_raw)
    l_gain2 = load(gain_moe_h, gain_moe)
    l_router = load(w_router_h, w_router)
    l_slots = load(slots_h, slots)
    l_wout = load(w_out_h, w_out)

    l_depths.wait()
    length0 = lengths_s[0]
    length1 = lengths_s[1]
    row = iota((TOKENS, TOKENS), 0)
    col = iota((TOKENS, TOKENS), 1)
    spread = jnp.concatenate([depths[...], depths[...]], axis=1)
    pos_lane = jnp.where(
        iota((1, TOKENS), 1) < TREE, spread[0:1, :] + length0, spread[1:2, :] + length1
    ).astype(F32)
    positions = jnp.sum(jnp.where(row == col, pos_lane, 0.0), axis=1, keepdims=True)
    lane = iota((1, HEAD), 1) % (HEAD // 2)
    freqs = jnp.exp(-jnp.log(jnp.float32(THETA)) * lane.astype(F32) / (HEAD // 2))
    angles = positions * freqs
    cosine = jnp.cos(angles)
    sine = jnp.sin(angles)
    sine = jnp.where(col < HEAD // 2, -sine, sine)

    def rotary(values):
        return values * cosine + pltpu.roll(values, HEAD // 2, 1) * sine

    l_drafts.wait()
    l_gain.wait()
    inputs = drafts[...].reshape(TOKENS, WIDTH).astype(F32)
    mean = jnp.mean(inputs * inputs, axis=-1, keepdims=True)
    normed = (inputs * lax.rsqrt(mean + EPSILON) * gain_attn[...]).astype(BF16)
    l_wq.wait()
    l_wk.wait()
    l_wv.wait()
    qkv = mm(normed, w_qkv[...])
    heads_q = [
        rotary(qkv[:, h * HEAD : (h + 1) * HEAD]).astype(BF16) for h in range(HEADS)
    ]
    key_new = rotary(qkv[:, QUARTER : QUARTER + HEAD]).astype(BF16)
    val_new = qkv[:, QUARTER + HEAD :].astype(BF16)

    scale = HEAD ** (-0.5)
    l_mask.wait()
    queries = []
    start = []
    for request in range(2):
        span = slice(request * TREE, (request + 1) * TREE)
        q = jnp.concatenate([part[span] for part in heads_q], axis=0)
        allowed = jnp.concatenate([tree_mask[request]] * HEADS, axis=0) > 0
        scores = jnp.where(allowed, mm_nt(q, key_new[span]) * scale, -jnp.inf)
        peak = jnp.max(scores, axis=1, keepdims=True)
        weights = jnp.exp(scores - peak)
        queries.append(q)
        start.append(
            (
                peak,
                jnp.sum(weights, axis=1, keepdims=True),
                mm(weights.astype(BF16), val_new[span]),
            )
        )
    for copy in l_cache:
        copy.wait()

    def step(block, carry):
        found = []
        for request in range(2):
            peak, total, accum = carry[request]
            span = pl.ds(pl.multiple_of(block * BLOCK, BLOCK), BLOCK)
            limit = length0 if request == 0 else length1
            inside = block * BLOCK + iota((1, BLOCK), 1) < limit
            scores = mm_nt(queries[request], kbuf[request, span, :]) * scale
            scores = jnp.where(inside, scores, -jnp.inf)
            peak_now = jnp.maximum(peak, jnp.max(scores, axis=1, keepdims=True))
            weights = jnp.exp(scores - peak_now)
            fade = jnp.exp(peak - peak_now)
            total = total * fade + jnp.sum(weights, axis=1, keepdims=True)
            accum = accum * fade + mm(weights.astype(BF16), vbuf[request, span, :])
            found.append((peak_now, total, accum))
        return tuple(found)

    done = lax.fori_loop(0, LONGEST // BLOCK, step, tuple(start))
    mixed = [(accum / total).astype(BF16) for unused, total, accum in done]
    heads = jnp.concatenate(
        [
            jnp.concatenate([part[h * TREE : (h + 1) * TREE] for part in mixed], axis=0)
            for h in range(HEADS)
        ],
        axis=1,
    )

    pl.semaphore_wait(barrier, PEERS)

    def quarter(index):
        return pl.ds(pl.multiple_of(index * QUARTER, QUARTER), QUARTER)

    l_wo.wait()
    rs_copies = {}
    for dx in (2, 1, 3):
        peer = (x + dx) % NX
        rs_send[dx - 1] = mm(heads, w_output[:, quarter(peer)]).astype(BF16)
        rs_copies[dx] = pltpu.make_async_remote_copy(
            src_ref=rs_send.at[dx - 1],
            dst_ref=rs_recv.at[dx - 1],
            send_sem=rs_ssem.at[dx - 1],
            recv_sem=rs_rsem.at[dx - 1],
            device_id=(req, peer),
            device_id_type=MESH,
        )
        rs_copies[dx].start()
    attn_own = mm(heads, w_output[:, quarter(x)])

    ord_all[0] = jnp.where(iota((8, HEAD), 1) < KEEP, order_s[0], order_s[1])
    ord_copies = []
    for dz in range(1, NZ):
        copy = pltpu.make_async_remote_copy(
            src_ref=ord_all.at[0],
            dst_ref=ord_all.at[dz],
            send_sem=ord_ssem.at[dz - 1],
            recv_sem=ord_rsem.at[dz - 1],
            device_id=place((z + dz) % NZ, y, core),
            device_id_type=MESH,
        )
        copy.start()
        ord_copies.append(copy)

    l_ids.wait()
    ids_lane = jnp.concatenate([ids[0], ids[1]], axis=1)
    expert = iota((CHIPS, TOKENS), 0)
    picked = ids_lane[0:1, :] == expert
    for choice in range(1, 4):
        picked = picked | (ids_lane[choice : choice + 1, :] == expert)
    picked_f = jnp.where(picked, 1.0, 0.0)
    before = jnp.where(row < col, 1.0, 0.0).astype(BF16)
    slot = mm(picked_f.astype(BF16), before).astype(jnp.int32) - x * SHARE
    slot = jnp.where(picked, slot, -1)
    hit = slot[:, None, :] == iota((CHIPS, SHARE, TOKENS), 1)
    hit_f = jnp.where(hit, 1.0, 0.0)
    dmat[...] = hit_f.reshape(CHIPS * SHARE, TOKENS).astype(BF16)

    l_win.wait()
    part_rows = 64

    def split(index, unused):
        span = pl.ds(pl.multiple_of(index * part_rows, part_rows), part_rows)
        block = w_in_raw[span]
        w_in[0, span, :] = block[:, 0, :]
        w_in[1, span, :] = block[:, 1, :]
        return 0

    lax.fori_loop(0, WIDTH // part_rows // 2, split, 0)

    for dx in (1, 3, 2):
        rs_copies[dx].wait_recv()
    for dx in range(1, NX):
        attn_own = attn_own + rs_recv[dx - 1].astype(F32)
    ag_all[x] = attn_own.astype(BF16)
    ag_copies = {}
    for dx in (2, 1, 3):
        ag_copies[dx] = pltpu.make_async_remote_copy(
            src_ref=ag_all.at[x],
            dst_ref=ag_all.at[x],
            send_sem=ag_ssem.at[dx - 1],
            recv_sem=ag_rsem.at[dx - 1],
            device_id=(req, (x + dx) % NX),
            device_id_type=MESH,
        )
        ag_copies[dx].start()

    lax.fori_loop(WIDTH // part_rows // 2, WIDTH // part_rows, split, 0)
    l_gain2.wait()
    for dx in (1, 3, 2):
        wait_for(ag_all.at[(x + NX - dx) % NX], ag_rsem.at[dx - 1])

    resid = jnp.concatenate(
        [
            drafts[:, :, j * QUARTER : (j + 1) * QUARTER].reshape(TOKENS, QUARTER).astype(F32)
            + ag_all[j].astype(F32)
            for j in range(NX)
        ],
        axis=1,
    )
    mean2 = jnp.mean(resid * resid, axis=-1, keepdims=True)
    normed2[...] = (resid * lax.rsqrt(mean2 + EPSILON) * gain_moe[...]).astype(BF16)

    for half in range(2):
        found = mm(dmat[half * TOKENS : (half + 1) * TOKENS, :], normed2[...])
        send_buf[half * 16 : (half + 1) * 16] = found.reshape(16, SHARE, WIDTH).astype(BF16)
    where = {}
    for index, pair in enumerate(BATCHES):
        for side, dz in enumerate(pair):
            where[dz] = (index, side * NY)
    own_send = pltpu.make_async_copy(send_buf.at[chip], rows.at[0, 0, 0], disp_rsem.at[0])
    own_send.start()
    for dz in SEND_ORDER:
        for dy in range(NY):
            if dz == 0 and dy == 0:
                continue
            batch, base = where[dz]
            zz = (z + dz) % NZ
            yy = (y + dy) % NY
            pltpu.make_async_remote_copy(
                src_ref=send_buf.at[zz * NY + yy],
                dst_ref=rows.at[batch, 0, base + dy],
                send_sem=disp_ssem,
                recv_sem=disp_rsem.at[batch],
                device_id=place(zz, yy, core),
                device_id_type=MESH,
            ).start()

    l_router.wait()
    logits = mm_nt(w_router[...], normed2[...])
    chosen = jnp.where(picked, jax.nn.sigmoid(logits), 0.0)
    gates = (chosen / jnp.sum(chosen, axis=0, keepdims=True)).astype(BF16).astype(F32)
    comb[...] = jnp.where(hit, gates[:, None, :], 0.0).reshape(CHIPS * SHARE, TOKENS).astype(BF16)

    l_wout.wait()
    relays = {}
    siblings = {}

    def relay(batch):
        wait_for(rows.at[batch, 0], disp_rsem.at[batch])
        copy = pltpu.make_async_remote_copy(
            src_ref=rows.at[batch, 0],
            dst_ref=rows.at[batch, 1],
            send_sem=relay_ssem.at[batch],
            recv_sem=relay_rsem.at[batch],
            device_id=place(z, y, other),
            device_id_type=MESH,
        )
        copy.start()
        relays[batch] = copy

    def experts(batch):
        relays[batch].wait_recv()
        held = to_rows(rows[batch])
        gate = mm(held, w_in[0])
        upper = mm(held, w_in[1])
        act = (jnp.maximum(gate, 0.0) * upper).astype(BF16)
        part = mm(act, w_out[...]).astype(BF16)
        own_part[batch] = part[:TREE].astype(F32)
        sib_send[batch] = part[TREE:]
        copy = pltpu.make_async_remote_copy(
            src_ref=sib_send.at[batch],
            dst_ref=sib_recv.at[batch],
            send_sem=sib_ssem.at[batch],
            recv_sem=sib_rsem.at[batch],
            device_id=place(z, y, other),
            device_id_type=MESH,
        )
        copy.start()
        siblings[batch] = copy

    def give_back(batch):
        siblings[batch].wait_recv()
        total = own_part[batch] + sib_recv[batch].astype(F32)
        ret_send[batch] = total.reshape(8, SHARE, WIDTH).astype(BF16)
        for side, dz in enumerate(BATCHES[batch]):
            for dy in range(NY):
                source = ret_send.at[batch, side * NY + dy]
                if dz == 0 and dy == 0:
                    pltpu.make_async_copy(source, ret.at[chip], ret_rsem).start()
                    continue
                pltpu.make_async_remote_copy(
                    src_ref=source,
                    dst_ref=ret.at[chip],
                    send_sem=ret_ssem,
                    recv_sem=ret_rsem,
                    device_id=place((z + NZ - dz) % NZ, (y + NY - dy) % NY, core),
                    device_id_type=MESH,
                ).start()

    turn = (1, 2, 3, 0)
    for position, batch in enumerate(turn):
        relay(batch)
        if position:
            give_back(turn[position - 1])
        experts(batch)
    give_back(turn[-1])

    wait_for(ret, ret_rsem)
    mix_copies = {}

    def mixture(index):
        return mm_tn(comb[...], to_rows(ret[:, :, quarter(index)]))

    for dx in (2, 1, 3):
        peer = (x + dx) % NX
        mix_send[dx - 1] = mixture(peer).astype(BF16)
        mix_copies[dx] = pltpu.make_async_remote_copy(
            src_ref=mix_send.at[dx - 1],
            dst_ref=mix_recv.at[dx - 1],
            send_sem=mix_ssem.at[dx - 1],
            recv_sem=mix_rsem.at[dx - 1],
            device_id=(req, peer),
            device_id_type=MESH,
        )
        mix_copies[dx].start()
    total = mixture(x)
    total = total + drafts[:, :, quarter(x)].reshape(TOKENS, QUARTER).astype(F32)
    total = total + ag_all[x].astype(F32)
    l_slots.wait()
    slots_two = jnp.concatenate([slots[...], slots[...]], axis=1)
    slots_lane = jnp.where(iota((1, TOKENS), 1) < TREE, slots_two[0:1, :], slots_two[1:2, :])
    pick_row = iota((2 * KEEP, TOKENS), 0)
    pick_col = iota((2 * KEEP, TOKENS), 1)
    selector = jnp.where(
        (pick_row // KEEP == pick_col // TREE) & (pick_row % KEEP == slots_lane), 1.0, 0.0
    ).astype(BF16)
    for dx in (1, 3, 2):
        mix_copies[dx].wait_recv()
    for dx in range(1, NX):
        total = total + mix_recv[dx - 1].astype(F32)
    tree_out = total.astype(BF16)
    tree_out_ref[...] = tree_out.reshape(2, TREE, QUARTER)

    z_all[0] = mm(selector, tree_out).astype(BF16)
    z_copies = []
    for dz in (4, 3, 5, 2, 6, 1, 7):
        copy = pltpu.make_async_remote_copy(
            src_ref=z_all.at[0],
            dst_ref=z_all.at[dz],
            send_sem=z_ssem.at[dz - 1],
            recv_sem=z_rsem.at[dz - 1],
            device_id=place((z + dz) % NZ, y, core),
            device_id_type=MESH,
        )
        copy.start()
        z_copies.append(copy)
    for copy in ord_copies:
        copy.wait_recv()
    out_row = iota((256, 2 * KEEP), 0)
    out_col = iota((256, 2 * KEEP), 1)
    same = out_row % KEEP == out_col % KEEP
    target = z * KEEP + out_row // KEEP
    for copy in z_copies:
        copy.wait_recv()
    posted = jnp.zeros((256, QUARTER), F32)
    for dz in range(NZ):
        hits = same & (ord_all[dz][0:1, 0 : 2 * KEEP] == target)
        posted = posted + mm(jnp.where(hits, 1.0, 0.0).astype(BF16), z_all[dz])
    yc_send[...] = posted.reshape(8, 2 * KEEP, QUARTER).astype(BF16)
    yc_copies = []
    for dy in (2, 1, 3, 0):
        for flip in range(2):
            yy = (y + dy) % NY
            cc = other if flip else core
            index = yy * 2 + cc
            if dy == 0 and flip == 0:
                continue
            copy = pltpu.make_async_remote_copy(
                src_ref=yc_send.at[index],
                dst_ref=yc_recv.at[dy * 2 + flip],
                send_sem=yc_ssem.at[dy * 2 + flip - 1],
                recv_sem=yc_rsem.at[dy * 2 + flip - 1],
                device_id=place(z, yy, cc),
                device_id_type=MESH,
            )
            copy.start()
            yc_copies.append(copy)
    kept = yc_send[y * 2 + core].astype(F32)

    for dx in range(1, NX):
        rs_copies[dx].wait_send()
        ag_copies[dx].wait_send()
        mix_copies[dx].wait_send()
    for copy in ord_copies + z_copies:
        copy.wait_send()
    wait_for(send_buf.at[pl.ds(0, CHIPS - 1)], disp_ssem)
    wait_for(ret.at[pl.ds(0, CHIPS - 1)], ret_ssem)
    for batch in range(4):
        relays[batch].wait_send()
        siblings[batch].wait_send()
    for copy in yc_copies:
        copy.wait()
    for index in range(1, 8):
        kept = kept + yc_recv[index].astype(F32)
    accepted_ref[...] = kept.astype(BF16).reshape(2, KEEP, QUARTER)


def on_device(
    drafts,
    gain_attn,
    w_query,
    key_value_weight,
    w_output,
    cache,
    lengths,
    tree_mask,
    depths,
    gain_moe,
    w_router,
    expert_ids,
    w_in,
    w_out,
    slots,
    order,
):
    any_space = pl.BlockSpec(memory_space=pl.ANY)
    scalars = pl.BlockSpec(memory_space=pltpu.SMEM)
    in_specs = [any_space] * 16
    in_specs[6] = scalars
    in_specs[15] = scalars
    vmem = pltpu.VMEM
    sem = pltpu.SemaphoreType.DMA
    i32 = jnp.int32
    scratch = [
        vmem((2, TREE, WIDTH), BF16),
        vmem((1, WIDTH), F32),
        vmem((WIDTH, 640), BF16),
        vmem((QUARTER, WIDTH), BF16),
        vmem((2, LONGEST, HEAD), BF16),
        vmem((2, LONGEST, HEAD), BF16),
        vmem((2, TREE, TREE), i32),
        vmem((2, TREE), i32),
        vmem((1, WIDTH), F32),
        vmem((CHIPS, WIDTH), BF16),
        vmem((2, 4, TREE), i32),
        vmem((WIDTH, 2, HALF_FF), BF16),
        vmem((2, WIDTH, HALF_FF), BF16),
        vmem((HALF_FF, WIDTH), BF16),
        vmem((2, TREE), i32),
        sem((20,)),
        vmem((3, TOKENS, QUARTER), BF16),
        vmem((3, TOKENS, QUARTER), BF16),
        sem((3,)),
        sem((3,)),
        vmem((4, TOKENS, QUARTER), BF16),
        sem((3,)),
        sem((3,)),
        vmem((256, TOKENS), BF16),
        vmem((256, TOKENS), BF16),
        vmem((TOKENS, WIDTH), BF16),
        vmem((CHIPS, SHARE, WIDTH), BF16),
        vmem((4, 2, 8, SHARE, WIDTH), BF16),
        vmem((4, TREE, WIDTH), F32),
        vmem((4, TREE, WIDTH), BF16),
        vmem((4, TREE, WIDTH), BF16),
        vmem((4, 8, SHARE, WIDTH), BF16),
        vmem((CHIPS, SHARE, WIDTH), BF16),
        sem,
        sem((4,)),
        sem((4,)),
        sem((4,)),
        sem((4,)),
        sem((4,)),
        sem,
        sem,
        vmem((3, TOKENS, QUARTER), BF16),
        vmem((3, TOKENS, QUARTER), BF16),
        sem((3,)),
        sem((3,)),
        vmem((NZ, 8, HEAD), i32),
        sem((7,)),
        sem((7,)),
        vmem((NZ, 2 * KEEP, QUARTER), BF16),
        sem((7,)),
        sem((7,)),
        vmem((8, 2 * KEEP, QUARTER), BF16),
        vmem((8, 2 * KEEP, QUARTER), BF16),
        sem((7,)),
        sem((7,)),
    ]
    return pl.pallas_call(
        layer,
        out_shape=(
            jax.ShapeDtypeStruct((2, TREE, QUARTER), BF16),
            jax.ShapeDtypeStruct((2, KEEP, QUARTER), BF16),
        ),
        in_specs=in_specs,
        out_specs=(pl.BlockSpec(memory_space=vmem), pl.BlockSpec(memory_space=vmem)),
        scratch_shapes=scratch,
        compiler_params=pltpu.CompilerParams(
            collective_id=0, has_side_effects=True, vmem_limit_bytes=56 * 1024 * 1024
        ),
    )(
        drafts,
        gain_attn.reshape(1, WIDTH),
        w_query,
        key_value_weight,
        w_output,
        cache,
        lengths,
        tree_mask,
        depths,
        gain_moe.reshape(1, WIDTH),
        w_router.T,
        expert_ids.transpose(0, 2, 1),
        w_in.reshape(WIDTH, 2, HALF_FF),
        w_out.reshape(HALF_FF, WIDTH),
        slots,
        order,
    )


def solution(mesh):
    placed = (
        P("req", None, None),
        P(),
        P(None, "tp"),
        P(),
        P("tp", None),
        P("req", None, None, None, None),
        P("req"),
        P("req", None, None),
        P("req", None),
        P(),
        P(),
        P("req", None, None),
        P("req", None, None, None),
        P("req", None, None),
        P("req", None),
        P("req"),
    )
    return jax.shard_map(
        on_device,
        mesh=mesh,
        in_specs=placed,
        out_specs=(P("req", None, "tp"), P("req", None, "tp")),
        check_vma=False,
    )
```

time: 329 us -> 92.3 us (0.28); the launches traced: 325 us -> 92.1 us
  waiting for transfers between devices: 118 us -> 0 us
  blocking collectives: 104 us -> 0 us
  Pallas kernels: 0 us -> 86 us
  matrix products: 45.4 us -> 0 us
  other arithmetic: 18.1 us -> 0 us
  between operations: 15.8 us -> 0.64 us
  local copies, waits for them, and re-layouts: 16.6 us -> 5.48 us
  starting transfers between devices: 6.94 us -> 0 us
    all_to_all x2 -> x0, blocking collectives: 104 us -> none  [the longest x1 52.1 us: on_device(): lax.all_to_all(posted.reshape(req_count, req_dev, KEEP, quarter), 'req',...]
    pallas_call x0 -> x1, Pallas kernels: none -> 86 us  [on_device(): pl.pallas_call(layer, out_shape=(jax.ShapeDtypeStruct((2, TREE, QUARTER),...]
    psum x1 -> x0, waiting for transfers between devices: 62.2 us -> none  [on_device(): lax.psum(jnp.dot(heads, w_output, preferred_element_type=jnp.float32).ast...]
    dot_general x38 -> x0, matrix products: 45.4 us -> none  [the longest x18 20.2 us: inner_rows(): lax.dot_general(left, right, (((1,), (1,)), ((), ())), preferred_element_...]
    all_to_all x1 -> x0, waiting for transfers between devices: 37.9 us -> none  [on_device(): lax.all_to_all(outbound, 'req', split_axis=0, concat_axis=0, tiled=True)]
    unnamed x3 -> x0, waiting for transfers between devices: 17.7 us -> none
    lt x16 -> x0, other arithmetic: 10.1 us -> none  [block_scores(): inside = offset + jnp.arange(block_len) < limit]
    all_to_all x1 -> x0, starting transfers between devices: 6.68 us -> none  [on_device(): lax.all_to_all(outbound, 'req', split_axis=0, concat_axis=0, tiled=True)]
  transfers between devices with their start and end apart: 3 -> 0, of which waited for: 3 -> 0; matrix products, arithmetic and copies ran while one was open for 1% -> 0% of each run, Pallas kernels for 0% -> 0%
where the time goes in v1:
time: 92.3 us; the launch traced here: 92.1 us
  Pallas kernels  86 us (93%)
  local copies, waits for them, and re-layouts  5.48 us (6%)
    pallas_call x1, Pallas kernels, on_device(): pl.pallas_call(layer, out_shape=(jax.ShapeDtypeStruct((2, TREE, QUARTER),...  86 us
    unnamed x2, local copies, waits for them, and re-layouts  2.89 us

profile of v1, /device:TPU:1, one launch (start us, length us, event | category | flops | bytes accessed | tf_op | source)
XLA Modules:
  0.0 92.1 jit_solution(8419015269673316485)
XLA Ops:
  0.6 1.3 %reshape.16.gain_attn_h = f32[1,1536]{1,0:T(1,128)} reshape(f32[1536]{0:T(1024)} %param.17) | data formatting | bytes 12288 | tf_op jit(solution)/shard_map/reshape | solution.py:665
  1.9 1.3 %reshape.17.gain_moe_h = f32[1,1536]{1,0:T(1,128)} reshape(f32[1536]{0:T(1024)} %param.25) | data formatting | bytes 12288 | tf_op jit(solution)/shard_map/reshape | solution.py:673
  3.2 86.0 %shard_map.167 = (bf16[2,64,384]{2,1,0:T(8,128)(2,1)}, bf16[2,16,384]{2,1,0:T(8,128)(2,1)}) custom-call(bf16[2,64,1536]{2,1,0:T(8,128)(2,1)} %drafts_h.1, f32[1,1536]{1,0:T(1,128)} %reshape.16.gain_attn_h, bf16[1536,384]{1,0:T(8,128)(2,1)} %w_query_h.1, bf16[1536,512]{1,0:T(8,128)(2,1)} %kv_weight_h.1, bf16[384,1536]{1,0:T(8,128)(2,1)} %w_output_h.1, ...), custom_call_target="tpu_custom_call" | custom-call | tf_op jit(solution)/shard_map/pallas_call | solution.py:651
  89.2 1.5 %copy.20 = bf16[2,64,384]{2,1,0:T(8,128)(2,1)} copy(bf16[2,64,384]{2,1,0:T(8,128)(2,1)} %get-tuple-element.4) | data formatting | bytes 196608
  90.7 1.3 %copy.21 = bf16[2,16,384]{2,1,0:T(8,128)(2,1)} copy(bf16[2,16,384]{2,1,0:T(8,128)(2,1)} %get-tuple-element.5) | data formatting | bytes 49152

commit v2 on v1

--- a/solution.py
+++ b/solution.py
@@ -20,7 +20,7 @@
 WIDTH = 1536
 QUARTER = 384
 LONGEST = 3072
-BLOCK = 512
+BLOCK = 1024
 HALF_FF = 384
 PEERS = 38
 BATCHES = ((0, 4), (1, 7), (2, 6), (3, 5))
@@ -97,14 +97,23 @@
     rs_recv,
     rs_ssem,
     rs_rsem,
-    ag_all,
-    ag_ssem,
-    ag_rsem,
+    score_buf,
+    stat_all,
+    stat_ssem,
+    stat_rsem,
+    logit_all,
+    logit_ssem,
+    logit_rsem,
     dmat,
     comb,
-    normed2,
     send_buf,
+    landed,
     rows,
+    xa_ssem,
+    xa_rsem,
+    ret_x,
+    xb_ssem,
+    xb_rsem,
     own_part,
     sib_send,
     sib_recv,
@@ -118,10 +127,7 @@
     sib_rsem,
     ret_ssem,
     ret_rsem,
-    mix_send,
-    mix_recv,
-    mix_ssem,
-    mix_rsem,
+    route,
     ord_all,
     ord_ssem,
     ord_rsem,
@@ -184,14 +190,6 @@
     for request in range(2):
         l_cache.append(load(cache_h.at[request, 0, kv_head], kbuf.at[request]))
         l_cache.append(load(cache_h.at[request, 1, kv_head], vbuf.at[request]))
-    l_wo = load(w_output_h, w_output)
-    l_ids = load(ids_h, ids)
-    l_win = load(w_in_h, w_in_raw)
-    l_gain2 = load(gain_moe_h, gain_moe)
-    l_router = load(w_router_h, w_router)
-    l_slots = load(slots_h, slots)
-    l_wout = load(w_out_h, w_out)
-
     l_depths.wait()
     length0 = lengths_s[0]
     length1 = lengths_s[1]
@@ -227,75 +225,98 @@
     key_new = rotary(qkv[:, QUARTER : QUARTER + HEAD]).astype(BF16)
     val_new = qkv[:, QUARTER + HEAD :].astype(BF16)
 
+    l_wo = load(w_output_h, w_output)
+    l_ids = load(ids_h, ids)
+    l_win = load(w_in_h, w_in_raw)
+    l_gain2 = load(gain_moe_h, gain_moe)
+    l_router = load(w_router_h, w_router)
+    l_slots = load(slots_h, slots)
+    l_wout = load(w_out_h, w_out)
+
     scale = HEAD ** (-0.5)
     l_mask.wait()
-    queries = []
-    start = []
-    for request in range(2):
-        span = slice(request * TREE, (request + 1) * TREE)
-        q = jnp.concatenate([part[span] for part in heads_q], axis=0)
-        allowed = jnp.concatenate([tree_mask[request]] * HEADS, axis=0) > 0
-        scores = jnp.where(allowed, mm_nt(q, key_new[span]) * scale, -jnp.inf)
-        peak = jnp.max(scores, axis=1, keepdims=True)
-        weights = jnp.exp(scores - peak)
-        queries.append(q)
-        start.append(
-            (
-                peak,
-                jnp.sum(weights, axis=1, keepdims=True),
-                mm(weights.astype(BF16), val_new[span]),
-            )
-        )
-    for copy in l_cache:
-        copy.wait()
-
-    def step(block, carry):
-        found = []
-        for request in range(2):
-            peak, total, accum = carry[request]
-            span = pl.ds(pl.multiple_of(block * BLOCK, BLOCK), BLOCK)
-            limit = length0 if request == 0 else length1
-            inside = block * BLOCK + iota((1, BLOCK), 1) < limit
-            scores = mm_nt(queries[request], kbuf[request, span, :]) * scale
-            scores = jnp.where(inside, scores, -jnp.inf)
-            peak_now = jnp.maximum(peak, jnp.max(scores, axis=1, keepdims=True))
-            weights = jnp.exp(scores - peak_now)
-            fade = jnp.exp(peak - peak_now)
-            total = total * fade + jnp.sum(weights, axis=1, keepdims=True)
-            accum = accum * fade + mm(weights.astype(BF16), vbuf[request, span, :])
-            found.append((peak_now, total, accum))
-        return tuple(found)
-
-    done = lax.fori_loop(0, LONGEST // BLOCK, step, tuple(start))
-    mixed = [(accum / total).astype(BF16) for unused, total, accum in done]
-    heads = jnp.concatenate(
-        [
-            jnp.concatenate([part[h * TREE : (h + 1) * TREE] for part in mixed], axis=0)
-            for h in range(HEADS)
-        ],
-        axis=1,
-    )
-
-    pl.semaphore_wait(barrier, PEERS)
 
     def quarter(index):
         return pl.ds(pl.multiple_of(index * QUARTER, QUARTER), QUARTER)
 
+    def lanes_max(values):
+        found = values[:, :HEAD]
+        for index in range(1, values.shape[1] // HEAD):
+            found = jnp.maximum(found, values[:, index * HEAD : (index + 1) * HEAD])
+        return found
+
+    def lanes_sum(values):
+        found = values[:, :HEAD]
+        for index in range(1, values.shape[1] // HEAD):
+            found = found + values[:, index * HEAD : (index + 1) * HEAD]
+        return found
+
+    def attend(request, limit):
+        own = slice(request * TREE, (request + 1) * TREE)
+        q = jnp.concatenate([part[own] for part in heads_q], axis=0)
+        allowed = jnp.concatenate([tree_mask[request]] * HEADS, axis=0) > 0
+        tree_scores = jnp.where(allowed, mm_nt(q, key_new[own]), -jnp.inf)
+        l_cache[2 * request].wait()
+
+        def score(block, running):
+            span = pl.ds(pl.multiple_of(block * BLOCK, BLOCK), BLOCK)
+            inside = block * BLOCK + iota((1, BLOCK), 1) < limit
+            scores = jnp.where(inside, mm_nt(q, kbuf[request, span, :]), -jnp.inf)
+            score_buf[:, span] = scores
+            return jnp.maximum(running, lanes_max(scores))
+
+        running = lax.fori_loop(
+            0, LONGEST // BLOCK, score, jnp.full((HEADS * TREE, HEAD), -jnp.inf, F32)
+        )
+        peak = jnp.maximum(
+            jnp.max(running, axis=1, keepdims=True), jnp.max(tree_scores, axis=1, keepdims=True)
+        )
+        tree_weights = jnp.exp((tree_scores - peak) * scale)
+        accum = mm(tree_weights.astype(BF16), val_new[own])
+        l_cache[2 * request + 1].wait()
+
+        def collect(block, carry):
+            total, accum = carry
+            span = pl.ds(pl.multiple_of(block * BLOCK, BLOCK), BLOCK)
+            weights = jnp.exp((score_buf[:, span] - peak) * scale)
+            accum = accum + mm(weights.astype(BF16), vbuf[request, span, :])
+            return total + lanes_sum(weights), accum
+
+        total, accum = lax.fori_loop(
+            0, LONGEST // BLOCK, collect, (jnp.zeros((HEADS * TREE, HEAD), F32), accum)
+        )
+        total = jnp.sum(total, axis=1, keepdims=True) + jnp.sum(
+            tree_weights, axis=1, keepdims=True
+        )
+        mixed = (accum / total).astype(BF16)
+        return jnp.concatenate(
+            [mixed[h * TREE : (h + 1) * TREE] for h in range(HEADS)], axis=1
+        )
+
+    rs_copies = {}
+    owns = []
+
+    def project(request, heads):
+        for dx in (2, 1, 3):
+            peer = (x + dx) % NX
+            rs_send[dx - 1, request] = mm(heads, w_output[:, quarter(peer)]).astype(BF16)
+            copy = pltpu.make_async_remote_copy(
+                src_ref=rs_send.at[dx - 1, request],
+                dst_ref=rs_recv.at[dx - 1, request],
+                send_sem=rs_ssem.at[dx - 1, request],
+                recv_sem=rs_rsem.at[dx - 1, request],
+                device_id=(req, peer),
+                device_id_type=MESH,
+            )
+            copy.start()
+            rs_copies[dx, request] = copy
+        owns.append(mm(heads, w_output[:, quarter(x)]))
+
+    heads0 = attend(0, length0)
+    pl.semaphore_wait(barrier, PEERS)
     l_wo.wait()
-    rs_copies = {}
-    for dx in (2, 1, 3):
-        peer = (x + dx) % NX
-        rs_send[dx - 1] = mm(heads, w_output[:, quarter(peer)]).astype(BF16)
-        rs_copies[dx] = pltpu.make_async_remote_copy(
-            src_ref=rs_send.at[dx - 1],
-            dst_ref=rs_recv.at[dx - 1],
-            send_sem=rs_ssem.at[dx - 1],
-            recv_sem=rs_rsem.at[dx - 1],
-            device_id=(req, peer),
-            device_id_type=MESH,
-        )
-        rs_copies[dx].start()
-    attn_own = mm(heads, w_output[:, quarter(x)])
+    project(0, heads0)
+    project(1, attend(1, length1))
 
     ord_all[0] = jnp.where(iota((8, HEAD), 1) < KEEP, order_s[0], order_s[1])
     ord_copies = []
@@ -319,11 +340,11 @@
         picked = picked | (ids_lane[choice : choice + 1, :] == expert)
     picked_f = jnp.where(picked, 1.0, 0.0)
     before = jnp.where(row < col, 1.0, 0.0).astype(BF16)
-    slot = mm(picked_f.astype(BF16), before).astype(jnp.int32) - x * SHARE
+    slot = mm(picked_f.astype(BF16), before).astype(jnp.int32)
     slot = jnp.where(picked, slot, -1)
-    hit = slot[:, None, :] == iota((CHIPS, SHARE, TOKENS), 1)
+    hit = slot[:, None, :] == iota((CHIPS, NX * SHARE, TOKENS), 1)
     hit_f = jnp.where(hit, 1.0, 0.0)
-    dmat[...] = hit_f.reshape(CHIPS * SHARE, TOKENS).astype(BF16)
+    dmat[...] = hit_f.reshape(CHIPS * NX * SHARE, TOKENS).astype(BF16)
 
     l_win.wait()
     part_rows = 64
@@ -335,49 +356,49 @@
         w_in[1, span, :] = block[:, 1, :]
         return 0
 
-    lax.fori_loop(0, WIDTH // part_rows // 2, split, 0)
-
-    for dx in (1, 3, 2):
-        rs_copies[dx].wait_recv()
-    for dx in range(1, NX):
-        attn_own = attn_own + rs_recv[dx - 1].astype(F32)
-    ag_all[x] = attn_own.astype(BF16)
-    ag_copies = {}
+    lax.fori_loop(0, WIDTH // part_rows, split, 0)
+    l_gain2.wait()
+
+    resid = []
+    for request in range(2):
+        for dx in (1, 3, 2):
+            rs_copies[dx, request].wait_recv()
+        found = owns[request] + drafts[request, :, quarter(x)].astype(F32)
+        for dx in range(1, NX):
+            found = found + rs_recv[dx - 1, request].astype(F32)
+        resid.append(found)
+    resid = jnp.concatenate(resid, axis=0)
+    squares = jnp.sum(resid * resid, axis=1, keepdims=True)
+    stat = jnp.sum(jnp.where(row == col, squares, 0.0), axis=0, keepdims=True)
+    stat_all[0] = jnp.broadcast_to(stat, (8, TOKENS))
+    stat_copies = []
     for dx in (2, 1, 3):
-        ag_copies[dx] = pltpu.make_async_remote_copy(
-            src_ref=ag_all.at[x],
-            dst_ref=ag_all.at[x],
-            send_sem=ag_ssem.at[dx - 1],
-            recv_sem=ag_rsem.at[dx - 1],
+        copy = pltpu.make_async_remote_copy(
+            src_ref=stat_all.at[0],
+            dst_ref=stat_all.at[dx],
+            send_sem=stat_ssem.at[dx - 1],
+            recv_sem=stat_rsem.at[dx - 1],
             device_id=(req, (x + dx) % NX),
             device_id_type=MESH,
         )
-        ag_copies[dx].start()
-
-    lax.fori_loop(WIDTH // part_rows // 2, WIDTH // part_rows, split, 0)
-    l_gain2.wait()
-    for dx in (1, 3, 2):
-        wait_for(ag_all.at[(x + NX - dx) % NX], ag_rsem.at[dx - 1])
-
-    resid = jnp.concatenate(
-        [
-            drafts[:, :, j * QUARTER : (j + 1) * QUARTER].reshape(TOKENS, QUARTER).astype(F32)
-            + ag_all[j].astype(F32)
-            for j in range(NX)
-        ],
-        axis=1,
-    )
-    mean2 = jnp.mean(resid * resid, axis=-1, keepdims=True)
-    normed2[...] = (resid * lax.rsqrt(mean2 + EPSILON) * gain_moe[...]).astype(BF16)
+        copy.start()
+        stat_copies.append(copy)
+    scaled = resid * gain_moe[:, quarter(x)]
+    for copy in stat_copies:
+        copy.wait_recv()
+    for dx in range(1, NX):
+        stat = stat + stat_all[dx][0:1, :]
+    squares = jnp.sum(jnp.where(row == col, stat, 0.0), axis=1, keepdims=True)
+    normed2 = (scaled * lax.rsqrt(squares / WIDTH + EPSILON)).astype(BF16)
 
     for half in range(2):
-        found = mm(dmat[half * TOKENS : (half + 1) * TOKENS, :], normed2[...])
-        send_buf[half * 16 : (half + 1) * 16] = found.reshape(16, SHARE, WIDTH).astype(BF16)
+        found = mm(dmat[half * 512 : (half + 1) * 512, :], normed2)
+        send_buf[half * 16 : (half + 1) * 16] = found.reshape(16, NX, SHARE, QUARTER).astype(BF16)
     where = {}
     for index, pair in enumerate(BATCHES):
         for side, dz in enumerate(pair):
             where[dz] = (index, side * NY)
-    own_send = pltpu.make_async_copy(send_buf.at[chip], rows.at[0, 0, 0], disp_rsem.at[0])
+    own_send = pltpu.make_async_copy(send_buf.at[chip], landed.at[0, 0], disp_rsem.at[0])
     own_send.start()
     for dz in SEND_ORDER:
         for dy in range(NY):
@@ -388,7 +409,7 @@
             yy = (y + dy) % NY
             pltpu.make_async_remote_copy(
                 src_ref=send_buf.at[zz * NY + yy],
-                dst_ref=rows.at[batch, 0, base + dy],
+                dst_ref=landed.at[batch, base + dy],
                 send_sem=disp_ssem,
                 recv_sem=disp_rsem.at[batch],
                 device_id=place(zz, yy, core),
@@ -396,17 +417,49 @@
             ).start()
 
     l_router.wait()
-    logits = mm_nt(w_router[...], normed2[...])
+    logit_all[0] = mm_nt(w_router[:, quarter(x)], normed2)
+    logit_copies = []
+    for dx in (2, 1, 3):
+        copy = pltpu.make_async_remote_copy(
+            src_ref=logit_all.at[0],
+            dst_ref=logit_all.at[dx],
+            send_sem=logit_ssem.at[dx - 1],
+            recv_sem=logit_rsem.at[dx - 1],
+            device_id=(req, (x + dx) % NX),
+            device_id_type=MESH,
+        )
+        copy.start()
+        logit_copies.append(copy)
+    for copy in logit_copies:
+        copy.wait_recv()
+    logits = (logit_all[0] + logit_all[1]) + (logit_all[2] + logit_all[3])
     chosen = jnp.where(picked, jax.nn.sigmoid(logits), 0.0)
     gates = (chosen / jnp.sum(chosen, axis=0, keepdims=True)).astype(BF16).astype(F32)
-    comb[...] = jnp.where(hit, gates[:, None, :], 0.0).reshape(CHIPS * SHARE, TOKENS).astype(BF16)
+    weighed = jnp.where(hit, gates[:, None, :], 0.0).reshape(CHIPS * NX * SHARE, TOKENS)
+    comb[...] = weighed.T.astype(BF16)
 
     l_wout.wait()
     relays = {}
     siblings = {}
 
+    def to_planes(batch):
+        wait_for(landed.at[batch], disp_rsem.at[batch])
+        pltpu.make_async_copy(
+            landed.at[batch, :, x], rows.at[batch, 0, x], xa_rsem.at[batch]
+        ).start()
+        for dx in (2, 1, 3):
+            peer = (x + dx) % NX
+            pltpu.make_async_remote_copy(
+                src_ref=landed.at[batch, :, peer],
+                dst_ref=rows.at[batch, 0, x],
+                send_sem=xa_ssem.at[batch],
+                recv_sem=xa_rsem.at[batch],
+                device_id=(req, peer),
+                device_id_type=MESH,
+            ).start()
+
     def relay(batch):
-        wait_for(rows.at[batch, 0], disp_rsem.at[batch])
+        wait_for(rows.at[batch, 0], xa_rsem.at[batch])
         copy = pltpu.make_async_remote_copy(
             src_ref=rows.at[batch, 0],
             dst_ref=rows.at[batch, 1],
@@ -420,7 +473,7 @@
 
     def experts(batch):
         relays[batch].wait_recv()
-        held = to_rows(rows[batch])
+        held = jnp.concatenate([to_rows(rows[batch, :, part]) for part in range(NX)], axis=1)
         gate = mm(held, w_in[0])
         upper = mm(held, w_in[1])
         act = (jnp.maximum(gate, 0.0) * upper).astype(BF16)
@@ -438,10 +491,31 @@
         copy.start()
         siblings[batch] = copy
 
-    def give_back(batch):
+    def from_planes(batch):
         siblings[batch].wait_recv()
         total = own_part[batch] + sib_recv[batch].astype(F32)
-        ret_send[batch] = total.reshape(8, SHARE, WIDTH).astype(BF16)
+        for part in range(NX):
+            ret_x[batch, part] = (
+                total[:, part * QUARTER : (part + 1) * QUARTER]
+                .reshape(8, SHARE, QUARTER)
+                .astype(BF16)
+            )
+        pltpu.make_async_copy(
+            ret_x.at[batch, x], ret_send.at[batch, :, x], xb_rsem.at[batch]
+        ).start()
+        for dx in (2, 1, 3):
+            peer = (x + dx) % NX
+            pltpu.make_async_remote_copy(
+                src_ref=ret_x.at[batch, peer],
+                dst_ref=ret_send.at[batch, :, x],
+                send_sem=xb_ssem.at[batch],
+                recv_sem=xb_rsem.at[batch],
+                device_id=(req, peer),
+                device_id_type=MESH,
+            ).start()
+
+    def give_back(batch):
+        wait_for(ret_send.at[batch], xb_rsem.at[batch])
         for side, dz in enumerate(BATCHES[batch]):
             for dy in range(NY):
                 source = ret_send.at[batch, side * NY + dy]
@@ -457,35 +531,28 @@
                     device_id_type=MESH,
                 ).start()
 
-    turn = (1, 2, 3, 0)
-    for position, batch in enumerate(turn):
-        relay(batch)
-        if position:
-            give_back(turn[position - 1])
-        experts(batch)
-    give_back(turn[-1])
-
-    wait_for(ret, ret_rsem)
-    mix_copies = {}
-
-    def mixture(index):
-        return mm_tn(comb[...], to_rows(ret[:, :, quarter(index)]))
-
-    for dx in (2, 1, 3):
-        peer = (x + dx) % NX
-        mix_send[dx - 1] = mixture(peer).astype(BF16)
-        mix_copies[dx] = pltpu.make_async_remote_copy(
-            src_ref=mix_send.at[dx - 1],
-            dst_ref=mix_recv.at[dx - 1],
-            send_sem=mix_ssem.at[dx - 1],
-            recv_sem=mix_rsem.at[dx - 1],
-            device_id=(req, peer),
-            device_id_type=MESH,
-        )
-        mix_copies[dx].start()
-    total = mixture(x)
-    total = total + drafts[:, :, quarter(x)].reshape(TOKENS, QUARTER).astype(F32)
-    total = total + ag_all[x].astype(F32)
+    first, second, third, fourth = 1, 2, 3, 0
+    to_planes(first)
+    relay(first)
+    to_planes(second)
+    experts(first)
+    from_planes(first)
+    relay(second)
+    to_planes(third)
+    experts(second)
+    give_back(first)
+    from_planes(second)
+    relay(third)
+    to_planes(fourth)
+    experts(third)
+    give_back(second)
+    from_planes(third)
+    relay(fourth)
+    experts(fourth)
+    give_back(third)
+    from_planes(fourth)
+    give_back(fourth)
+
     l_slots.wait()
     slots_two = jnp.concatenate([slots[...], slots[...]], axis=1)
     slots_lane = jnp.where(iota((1, TOKENS), 1) < TREE, slots_two[0:1, :], slots_two[1:2, :])
@@ -494,11 +561,20 @@
     selector = jnp.where(
         (pick_row // KEEP == pick_col // TREE) & (pick_row % KEEP == slots_lane), 1.0, 0.0
     ).astype(BF16)
-    for dx in (1, 3, 2):
-        mix_copies[dx].wait_recv()
-    for dx in range(1, NX):
-        total = total + mix_recv[dx - 1].astype(F32)
-    tree_out = total.astype(BF16)
+    for copy in ord_copies:
+        copy.wait_recv()
+    out_row = iota((256, 2 * KEEP), 0)
+    out_col = iota((256, 2 * KEEP), 1)
+    same = out_row % KEEP == out_col % KEEP
+    target = z * KEEP + out_row // KEEP
+    hits = [
+        jnp.where(same & (ord_all[dz][0:1, 0 : 2 * KEEP] == target), 1.0, 0.0)
+        for dz in range(NZ)
+    ]
+    route[...] = jnp.concatenate(hits, axis=1).astype(BF16)
+
+    wait_for(ret, ret_rsem)
+    tree_out = (resid + mm(comb[...], to_rows(ret[...]))).astype(BF16)
     tree_out_ref[...] = tree_out.reshape(2, TREE, QUARTER)
 
     z_all[0] = mm(selector, tree_out).astype(BF16)
@@ -514,18 +590,9 @@
         )
         copy.start()
         z_copies.append(copy)
-    for copy in ord_copies:
-        copy.wait_recv()
-    out_row = iota((256, 2 * KEEP), 0)
-    out_col = iota((256, 2 * KEEP), 1)
-    same = out_row % KEEP == out_col % KEEP
-    target = z * KEEP + out_row // KEEP
     for copy in z_copies:
         copy.wait_recv()
-    posted = jnp.zeros((256, QUARTER), F32)
-    for dz in range(NZ):
-        hits = same & (ord_all[dz][0:1, 0 : 2 * KEEP] == target)
-        posted = posted + mm(jnp.where(hits, 1.0, 0.0).astype(BF16), z_all[dz])
+    posted = mm(route[...], z_all[...].reshape(256, QUARTER))
     yc_send[...] = posted.reshape(8, 2 * KEEP, QUARTER).astype(BF16)
     yc_copies = []
     for dy in (2, 1, 3, 0):
@@ -547,17 +614,15 @@
             yc_copies.append(copy)
     kept = yc_send[y * 2 + core].astype(F32)
 
-    for dx in range(1, NX):
-        rs_copies[dx].wait_send()
-        ag_copies[dx].wait_send()
-        mix_copies[dx].wait_send()
-    for copy in ord_copies + z_copies:
+    for copy in list(rs_copies.values()) + stat_copies + logit_copies + ord_copies + z_copies:
         copy.wait_send()
     wait_for(send_buf.at[pl.ds(0, CHIPS - 1)], disp_ssem)
     wait_for(ret.at[pl.ds(0, CHIPS - 1)], ret_ssem)
     for batch in range(4):
         relays[batch].wait_send()
         siblings[batch].wait_send()
+        wait_for(rows.at[batch, 0, pl.ds(0, NX - 1)], xa_ssem.at[batch])
+        wait_for(ret_x.at[batch, pl.ds(0, NX - 1)], xb_ssem.at[batch])
     for copy in yc_copies:
         copy.wait()
     for index in range(1, 8):
@@ -608,23 +673,32 @@
         vmem((HALF_FF, WIDTH), BF16),
         vmem((2, TREE), i32),
         sem((20,)),
-        vmem((3, TOKENS, QUARTER), BF16),
-        vmem((3, TOKENS, QUARTER), BF16),
+        vmem((3, 2, TREE, QUARTER), BF16),
+        vmem((3, 2, TREE, QUARTER), BF16),
+        sem((3, 2)),
+        sem((3, 2)),
+        vmem((HEADS * TREE, LONGEST), F32),
+        vmem((NX, 8, TOKENS), F32),
         sem((3,)),
         sem((3,)),
-        vmem((4, TOKENS, QUARTER), BF16),
+        vmem((NX, CHIPS, TOKENS), F32),
         sem((3,)),
         sem((3,)),
-        vmem((256, TOKENS), BF16),
-        vmem((256, TOKENS), BF16),
-        vmem((TOKENS, WIDTH), BF16),
-        vmem((CHIPS, SHARE, WIDTH), BF16),
-        vmem((4, 2, 8, SHARE, WIDTH), BF16),
+        vmem((CHIPS * NX * SHARE, TOKENS), BF16),
+        vmem((TOKENS, CHIPS * NX * SHARE), BF16),
+        vmem((CHIPS, NX, SHARE, QUARTER), BF16),
+        vmem((4, 8, NX, SHARE, QUARTER), BF16),
+        vmem((4, 2, NX, 8, SHARE, QUARTER), BF16),
+        sem((4,)),
+        sem((4,)),
+        vmem((4, NX, 8, SHARE, QUARTER), BF16),
+        sem((4,)),
+        sem((4,)),
         vmem((4, TREE, WIDTH), F32),
         vmem((4, TREE, WIDTH), BF16),
         vmem((4, TREE, WIDTH), BF16),
-        vmem((4, 8, SHARE, WIDTH), BF16),
-        vmem((CHIPS, SHARE, WIDTH), BF16),
+        vmem((4, 8, NX, SHARE, QUARTER), BF16),
+        vmem((CHIPS, NX, SHARE, QUARTER), BF16),
         sem,
         sem((4,)),
         sem((4,)),
@@ -633,10 +707,7 @@
         sem((4,)),
         sem,
         sem,
-        vmem((3, TOKENS, QUARTER), BF16),
-        vmem((3, TOKENS, QUARTER), BF16),
-        sem((3,)),
-        sem((3,)),
+        vmem((256, 256), BF16),
         vmem((NZ, 8, HEAD), i32),
         sem((7,)),
         sem((7,)),

time: 92.3 us -> 89.8 us (0.973)
  Pallas kernels: 86 us -> 83.4 us
    pallas_call x1, Pallas kernels: 86 us -> 83.4 us  [on_device(): pl.pallas_call(layer, out_shape=(jax.ShapeDtypeStruct((2, TREE, QUARTER),...]
where the time goes in v2:
time: 89.8 us; the launch traced here: 89.5 us
  Pallas kernels  83.4 us (93%)
  local copies, waits for them, and re-layouts  5.48 us (6%)
    pallas_call x1, Pallas kernels, on_device(): pl.pallas_call(layer, out_shape=(jax.ShapeDtypeStruct((2, TREE, QUARTER),...  83.4 us
    unnamed x2, local copies, waits for them, and re-layouts  2.89 us

profile of v2, /device:TPU:1, one launch (start us, length us, event | category | flops | bytes accessed | tf_op | source)
XLA Modules:
  0.0 89.5 jit_solution(2465390990986060173)
XLA Ops:
  0.6 1.3 %reshape.16.gain_attn_h = f32[1,1536]{1,0:T(1,128)} reshape(f32[1536]{0:T(1024)} %param.17) | data formatting | bytes 12288 | tf_op jit(solution)/shard_map/reshape | solution.py:736
  1.9 1.3 %reshape.17.gain_moe_h = f32[1,1536]{1,0:T(1,128)} reshape(f32[1536]{0:T(1024)} %param.25) | data formatting | bytes 12288 | tf_op jit(solution)/shard_map/reshape | solution.py:744
  3.2 83.4 %shard_map.167 = (bf16[2,64,384]{2,1,0:T(8,128)(2,1)}, bf16[2,16,384]{2,1,0:T(8,128)(2,1)}) custom-call(bf16[2,64,1536]{2,1,0:T(8,128)(2,1)} %drafts_h.1, f32[1,1536]{1,0:T(1,128)} %reshape.16.gain_attn_h, bf16[1536,384]{1,0:T(8,128)(2,1)} %w_query_h.1, bf16[1536,512]{1,0:T(8,128)(2,1)} %kv_weight_h.1, bf16[384,1536]{1,0:T(8,128)(2,1)} %w_output_h.1, ...), custom_call_target="tpu_custom_call" | custom-call | tf_op jit(solution)/shard_map/pallas_call | solution.py:722
  86.6 1.5 %copy.20 = bf16[2,64,384]{2,1,0:T(8,128)(2,1)} copy(bf16[2,64,384]{2,1,0:T(8,128)(2,1)} %get-tuple-element.4) | data formatting | bytes 196608
  88.2 1.3 %copy.21 = bf16[2,16,384]{2,1,0:T(8,128)(2,1)} copy(bf16[2,16,384]{2,1,0:T(8,128)(2,1)} %get-tuple-element.5) | data formatting | bytes 49152
